TPU v7x, 128 devices: a whole 4x4x4 slice. The times are simulated.
128 devices in a mesh: mesh: 2 (over core), blk: 64 (over y, x, z).
Axes of the slice: x: 4, y: 4, z: 4, core: 2. Of those that a mesh axis runs over, the one named last changes fastest.
Arguments:
- rotation_step: int32 [1], replicated, may hold values from 1 to 7
- field_state: float32 [2, 64, 4, 128, 256], P('mesh', 'blk'), may hold values from -6 to 6
- diffusivity: float32 [2, 64, 2, 128, 256], P('mesh', 'blk'), may hold values from 0.05 to 2
- stretch: float32 [2, 64, 128, 256], P('mesh', 'blk'), may hold values from 100 to 3000
- donor_base: int32 [2, 64, 4096], P('mesh', 'blk'), may hold values from 0 to 32478, as said below
- donor_frac: float32 [2, 64, 3, 4096], P('mesh', 'blk'), may hold values from 0 to 1
- fringe_cell: int32 [2, 64, 4096], P('mesh', 'blk'), may hold values from 0 to 32768, as said below
Outputs:
- new_fields: float32 [2, 64, 4, 128, 256], P('mesh', 'blk')
Inputs may be any that keep to these rules, and one draw needn't show every extreme that they name: `donor_base`: each entry is z * 8 * 32 + x * 32 + y with z < 127, x < 7 and y < 31. `fringe_cell`: in each block, the slots p * 64 to (p + 1) * 64 - 1 hold the cells that receive values from block p of the other mesh, used slots first; every fringe cell of the block is named by exactly one used slot; an unused slot holds 32768. A group has 0 to 64 used slots, and in every block some group is full and some is empty.
All inputs are finite; a program needn't handle non-finite values.
Results may differ from a plain program's by a relative error of at most 0.00017.
Values sent between devices are 32-bit elements; how exact they have to be, the bound alone decides.
A program may use at most 64 MiB of HBM per device.

v0:
```python
import functools

import jax
import jax.numpy as jnp
from jax import lax
from jax.experimental import pallas as pl
from jax.experimental.pallas import tpu as pltpu
from jax.sharding import PartitionSpec as P

CX, CY, CZ = 8, 32, 128
PLANE = CX * CY
ITERS = 2
TURN_MOST = 7
CAP = 64
TILE = 1024
LANES = 128
PITCH = 132
MESH = pl.DeviceIdType.MESH
BF = jnp.bfloat16
F32 = jnp.float32


def iota(shape, dim):
    return lax.broadcasted_iota(jnp.int32, shape, dim)


def kernel(
    rot, n,
    fs, kap, st, db, df, fc, out,
    F0, KV, SV, SB, SF, SC, A3, WH, WL, WZ, ZO, QO, QV, E, NN, V2,
    EP, CS, IN, R, G, D, V, FR, NS, EARLY, GOT, LATE,
    sendS, recvS, sendH, recvH,
    in_sem, s_sem, r_sem, hs_sem, hr_sem, m_sem,
):
    m = lax.axis_index("mesh")
    d = lax.axis_index("blk")
    slots = n * CAP
    tiles = slots // TILE
    right, left = lax.rem(d + 1, n), lax.rem(d + n - 1, n)
    ahead, back = lax.rem(d + rot, n), lax.rem(d + n - rot, n)

    loads = [
        pltpu.make_async_copy(src, dst, in_sem.at[i])
        for i, (src, dst) in enumerate(((db, SB), (df, SF), (fc, SC), (fs, F0), (kap, KV), (st, SV)))
    ]
    for copy in loads:
        copy.start()

    barrier = pltpu.get_barrier_semaphore()
    for peer in (left, right, ahead, back):
        pl.semaphore_signal(barrier, inc=1, device_id=(m, peer), device_id_type=MESH)

    @pl.loop(0, n // 16)
    def _(i):
        for u in range(16):
            peer = lax.rem(d + i * 16 + u, n)
            pl.semaphore_signal(barrier, inc=1, device_id=(1 - m, peer), device_id_type=MESH)

    row, col = iota((128, 2 * 2 * 4 * LANES), 0), iota((128, 2 * 2 * 4 * LANES), 1)
    q = row & 15
    kind, half, fld, lane = col >> 10, (col >> 9) & 1, (col >> 7) & 3, col & 127
    place = (q >> 1) * CY + (q & 1) * (CY - 1) + kind * (1 - 2 * (q & 1))
    E[...] = jnp.where((((row >> 4) & 3) == fld) & (half * LANES + lane == place), 1.0, 0.0).astype(BF)
    src, dst = iota((512, 256), 0) & 255, iota((512, 256), 1)
    gap = jnp.abs(src - dst)
    sy, dy = src & 31, dst & 31
    edge = (sy == 0) | (sy == CY - 1) | (dy == 0) | (dy == CY - 1)
    NN[...] = jnp.where(((gap == 1) | (gap == CY)) & ~edge, 1.0, 0.0).astype(BF)

    for copy in loads[:3]:
        copy.wait()
    turn = (slots - rot * CAP) % slots

    def turned(ref, i):
        x = ref[:, i * slots : (i + 1) * slots]
        return jnp.where(m == 0, pltpu.roll(x, turn, axis=1), x)

    for ref, count in ((SB, 1), (SC, 1), (SF, 3)):
        for i in range(count):
            ref[:, i * slots : (i + 1) * slots] = turned(ref, i)

    @pl.loop(0, slots // 256)
    def _(t):
        cols = pl.ds(pl.multiple_of(t * 256, 256), 256)
        b = SB[:, cols]
        fz, fx, fy = (SF[:, pl.ds(pl.multiple_of(i * slots + t * 256, 256), 256)] for i in range(3))
        z, x, y = b >> 8, (b >> 5) & 7, b & 31

        def hat(count, at, frac):
            i = iota((count, 256), 0)
            return jnp.where(i == at, 1.0 - frac, jnp.where(i == at + 1, frac, 0.0))

        hx, hy = hat(CX, x, fx), hat(CY, y, fy)
        for i in range(CX):
            w = hx[i : i + 1] * hy
            hi = w.astype(BF)
            WH[i * CY : (i + 1) * CY, cols] = hi
            WL[i * CY : (i + 1) * CY, cols] = (w - hi.astype(F32)).astype(BF)
        WZ[:, cols] = hat(CZ, z, fz)
        c = SC[:, cols]
        ZO[:, cols] = jnp.where(iota((CZ, 256), 0) == (c >> 8), 1.0, 0.0).astype(BF)
        cq = ((c >> 5) & 7) * 2 + jnp.where((c & 31) == 0, 0, 1)
        QO[:, cols] = jnp.where(iota((16, 256), 0) == cq, 1.0, 0.0)

    def split(h, x):
        hi = x.astype(BF)
        A3[:, h * LANES : (h + 1) * LANES] = hi
        A3[:, PLANE + h * LANES : PLANE + (h + 1) * LANES] = (x - hi.astype(F32)).astype(BF)
        A3[:, 2 * PLANE + h * LANES : 2 * PLANE + (h + 1) * LANES] = hi

    lane1 = iota((CZ, LANES), 1)

    def pack(it, get):
        sl, sr = get(0, 0), pltpu.roll(get(1, 0), 32, axis=1)
        for f in range(1, 4):
            here = (lane1 >> 5) == f
            sl = jnp.where(here, pltpu.roll(get(0, f), 32 * f, axis=1), sl)
            sr = jnp.where(here, pltpu.roll(get(1, f), (32 * f + 32) % 128, axis=1), sr)
        sendH[it, 0] = sl
        sendH[it, 1] = sr

    y4 = lane1 & 31
    fringe = (y4 == 0) | (y4 == CY - 1)

    def new(h, f):
        return jnp.where(fringe, FR[rows_of(h, f)], V[rows_of(h, f)])

    def rows_of(h, f):
        return slice((h * 4 + f) * PITCH, (h * 4 + f) * PITCH + CZ)

    def at(z):
        return pl.ds(z, 8, stride=PITCH)

    top, low = CZ // 2 - 1, CZ // 2

    def solve():
        def forward(i, carry):
            a, b = carry
            for u in range(8):
                z = i * 8 + u
                a = (R[at(z)] + a) * G[at(z)]
                b = (R[at(CZ - 1 - z)] + b) * G[at(CZ - 1 - z)]
                D[at(z)] = a
                D[at(CZ - 1 - z)] = b
            return a, b

        zero = jnp.zeros((8, LANES), F32)
        a, b = lax.fori_loop(0, CZ // 16, forward, (zero, zero))
        a = (a + G[at(top)] * b) * LATE[CZ : CZ + 8]
        b = b + G[at(low)] * a
        V[at(top)] = a
        V[at(low)] = b

        def backward(i, carry):
            a, b = carry
            for u in range(9):
                z = i * 9 + u + 1
                a = D[at(top - z)] + G[at(top - z)] * a
                b = D[at(low + z)] + G[at(low + z)] * b
                V[at(top - z)] = a
                V[at(low + z)] = b
            return a, b

        lax.fori_loop(0, 7, backward, (a, b))

    loads[3].wait()
    pack(0, lambda h, f: F0[f * CZ : (f + 1) * CZ, h * LANES : (h + 1) * LANES])
    for h in range(2):
        split(h, F0[:, h * LANES : (h + 1) * LANES])

    pl.semaphore_wait(barrier, n + 4)

    early = pltpu.make_async_remote_copy(
        src_ref=EARLY, dst_ref=GOT, send_sem=m_sem.at[0], recv_sem=m_sem.at[1],
        device_id=(m, ahead), device_id_type=MESH,
    )
    late = pltpu.make_async_remote_copy(
        src_ref=LATE.at[pl.ds(0, CZ)], dst_ref=LATE.at[pl.ds(CZ + 8, CZ)], send_sem=m_sem.at[2], recv_sem=m_sem.at[3],
        device_id=(m, ahead), device_id_type=MESH,
    )

    @pl.loop(0, ITERS)
    def _(it):
        halos = [
            pltpu.make_async_remote_copy(
                src_ref=sendH.at[it, e], dst_ref=recvH.at[it, e],
                send_sem=hs_sem.at[it, e], recv_sem=hr_sem.at[it, e],
                device_id=(m, left if e == 0 else right), device_id_type=MESH,
            )
            for e in range(2)
        ]
        for copy in halos:
            copy.start()

        per = TILE // CAP

        def send(t):
            tile = lax.rem(t + d // per, tiles)
            for i in range(per):
                pi = lax.rem(i + d, per)
                pltpu.make_async_remote_copy(
                    src_ref=sendS.at[it, i % 2, tile * (per // 2) + pi // 2], dst_ref=recvS.at[it, d],
                    send_sem=s_sem.at[it], recv_sem=r_sem.at[it],
                    device_id=(1 - m, tile * per + pi), device_id_type=MESH,
                ).start()

        @pl.loop(0, tiles)
        def _(t):
            tile = lax.rem(t + d // per, tiles)
            cols = pl.ds(pl.multiple_of(tile * TILE, TILE), TILE)

            @pl.when(t > 0)
            def _():
                send(t - 1)

            wh = WH[:, cols]
            p = jnp.dot(A3[...], jnp.concatenate([wh, wh, WL[:, cols]], axis=0), preferred_element_type=F32)
            s = jnp.sum(p.reshape(4, CZ, TILE) * WZ[:, cols][None], axis=1)
            for i in range(per // 2):
                x = s[:, i * LANES : (i + 1) * LANES]
                sendS[it, 0, tile * (per // 2) + i] = x
                sendS[it, 1, tile * (per // 2) + i] = pltpu.roll(x, CAP, axis=1)

        send(tiles - 1)

        @pl.when(it == 0)
        def _():
            loads[4].wait()
            loads[5].wait()
            for h in range(2):
                lanes = slice(h * LANES, (h + 1) * LANES)
                inv = 1.0 / SV[:, lanes]
                for f in range(4):
                    k = f // 3
                    c = KV[k * CZ : (k + 1) * CZ, lanes]
                    EP[rows_of(h, f)] = (1.0 + 4.0 * c) * inv
                    CS[rows_of(h, f)] = c * inv
                    IN[rows_of(h, f)] = F0[f * CZ : (f + 1) * CZ, lanes] * inv

            def factor(i, carry):
                ha, hb = carry
                for u in range(8):
                    z = i * 8 + u
                    ta, tb = EP[at(z)] + ha, EP[at(CZ - 1 - z)] + hb
                    ga, gb = 1.0 / (1.0 + ta), 1.0 / (1.0 + tb)
                    G[at(z)] = ga
                    G[at(CZ - 1 - z)] = gb
                    ha, hb = ta * ga, tb * gb
                return ha, hb

            one = jnp.ones((8, LANES), F32)
            ha, hb = lax.fori_loop(0, CZ // 16, factor, (one, one))
            LATE[CZ : CZ + 8] = 1.0 / (ha + hb - ha * hb)

        NS[...] = jnp.dot(A3[:, : 2 * PLANE], NN[...], preferred_element_type=F32)
        for copy in halos:
            copy.wait()
        hr, hl = recvH[it, 0], recvH[it, 1]
        for h in range(2):
            for f in range(4):
                x = NS[f * CZ : (f + 1) * CZ, h * LANES : (h + 1) * LANES]
                if h == 0:
                    x = x + jnp.where(lane1 < 32, pltpu.roll(hl, (128 - 32 * f) % 128, axis=1), 0.0)
                else:
                    x = x + jnp.where(lane1 >= 96, pltpu.roll(hr, 96 - 32 * f, axis=1), 0.0)
                R[rows_of(h, f)] = IN[rows_of(h, f)] + CS[rows_of(h, f)] * x

        @pl.when((it == ITERS - 1) & (m == 1))
        def _():
            solve()
            for h in range(2):
                for f in range(4):
                    EARLY[f * CZ : (f + 1) * CZ, h * LANES : (h + 1) * LANES] = V[rows_of(h, f)]
            early.start()

        pltpu.make_async_copy(recvS.at[it], recvS.at[it], r_sem.at[it]).wait()
        got = recvS[it].reshape(n // 2, 2, 4, LANES)
        v = jnp.where(iota((n // 2, 4, LANES), 2) < CAP, got[:, 0], got[:, 1])
        for i in range(n // 2):
            V2[:, i * LANES : (i + 1) * LANES] = v[i]
        rest = V2[...]
        for piece in range(2):
            part = rest.astype(BF).astype(F32)
            rest = rest - part
            for f in range(4):
                QV[piece * 64 + f * 16 : piece * 64 + f * 16 + 16, :] = (QO[...] * part[f : f + 1]).astype(BF)
        dp = lax.dot_general(ZO[...], QV[...], (((1,), (1,)), ((), ())), preferred_element_type=F32).astype(BF)
        for h in range(2):
            fr = jnp.dot(dp, E[:, h * 512 : (h + 1) * 512], preferred_element_type=F32)
            nb = jnp.dot(dp, E[:, 1024 + h * 512 : 1024 + (h + 1) * 512], preferred_element_type=F32)
            for f in range(4):
                FR[rows_of(h, f)] = fr[:, f * LANES : (f + 1) * LANES]
                R[rows_of(h, f)] = R[rows_of(h, f)] + CS[rows_of(h, f)] * nb[:, f * LANES : (f + 1) * LANES]
        solve()

        pltpu.make_async_copy(recvS.at[it], recvS.at[it], s_sem.at[it]).wait()

        @pl.when(it < ITERS - 1)
        def _():
            pack(it + 1, new)
            for h in range(2):
                split(h, jnp.concatenate([new(h, f) for f in range(4)], axis=0))

    @pl.when(m == 0)
    def _():
        for h in range(2):
            for f in range(4):
                out[f * CZ : (f + 1) * CZ, h * LANES : (h + 1) * LANES] = new(h, f)

    @pl.when(m == 1)
    def _():
        yy = lane1 & 3
        pick = ((lane1 >> 2) & 3) * CY + yy + jnp.where(yy >= 2, CY - 4, 0)
        acc = jnp.zeros((CZ, LANES), F32)
        for h in range(2):
            for f in range(4):
                x = jnp.take_along_axis(new(h, f), pick, axis=1, mode="promise_in_bounds")
                acc = jnp.where((lane1 >> 4) == f * 2 + h, x, acc)
        LATE[:CZ] = acc
        late.start()
        early.wait()
        late.wait()
        tail = LATE[CZ + 8 :]
        y = lane1 & 31
        home = (lane1 >> 5) * 4 + (y & 3)
        rim = (y < 2) | (y >= CY - 2)
        for h in range(2):
            for f in range(4):
                x = jnp.take_along_axis(tail, home + (f * 32 + h * 16), axis=1, mode="promise_in_bounds")
                block = (slice(f * CZ, (f + 1) * CZ), slice(h * LANES, (h + 1) * LANES))
                out[block] = jnp.where(rim, x, GOT[block])


def step(rot, n, args):
    slots = n * CAP
    vm = pltpu.VMEM
    dma = pltpu.SemaphoreType.DMA
    tall = vm((8 * PITCH, LANES), F32)
    return pl.pallas_call(
        functools.partial(kernel, rot, n),
        out_shape=jax.ShapeDtypeStruct((4 * CZ, PLANE), F32),
        in_specs=[pl.BlockSpec(memory_space=pl.ANY)] * 6,
        out_specs=pl.BlockSpec(memory_space=pltpu.VMEM),
        scratch_shapes=[
            vm((512, 256), F32), vm((256, 256), F32), vm((128, 256), F32),
            vm((1, slots), jnp.int32), vm((1, 3 * slots), F32), vm((1, slots), jnp.int32),
            vm((512, 768), BF), vm((256, slots), BF), vm((256, slots), BF), vm((CZ, slots), F32), vm((CZ, slots), BF),
            vm((16, slots), F32), vm((128, slots), BF), vm((128, 2048), BF), vm((512, 256), BF),
            vm((4, slots), F32),
            tall, tall, tall, tall, tall, tall, tall, tall,
            vm((512, 256), F32), vm((512, 256), F32), vm((512, 256), F32), vm((2 * CZ + 8, LANES), F32),
            vm((ITERS, 2, n // 2, 4, LANES), F32), vm((ITERS, n, 4, LANES), F32),
            vm((ITERS, 2, CZ, LANES), F32), vm((ITERS, 2, CZ, LANES), F32),
            dma((6,)), dma((ITERS,)), dma((ITERS,)), dma((ITERS, 2)), dma((ITERS, 2)), dma((4,)),
        ],
        compiler_params=pltpu.CompilerParams(collective_id=rot, has_side_effects=True),
        name=f"rotor_step_{rot}",
    )(*args)


def solution(mesh):
    n = mesh.shape["blk"]

    def local(rotation_step, field_state, diffusivity, stretch, donor_base, donor_frac, fringe_cell):
        slots = n * CAP
        args = (
            field_state.reshape(4 * CZ, PLANE),
            diffusivity.reshape(2 * CZ, PLANE),
            stretch.reshape(CZ, PLANE),
            donor_base.reshape(1, slots),
            donor_frac.reshape(1, 3 * slots),
            fringe_cell.reshape(1, slots),
        )
        branches = [functools.partial(lambda rot, a: step(rot, n, a), rot) for rot in range(1, TURN_MOST + 1)]
        new = lax.switch(jnp.clip(rotation_step[0] - 1, 0, TURN_MOST - 1), branches, args)
        return new.reshape(1, 1, 4, CZ, PLANE)

    placed = (
        P(),
        P("mesh", "blk", None, None, None),
        P("mesh", "blk", None, None, None),
        P("mesh", "blk", None, None),
        P("mesh", "blk", None),
        P("mesh", "blk", None, None),
        P("mesh", "blk", None),
    )
    return jax.shard_map(
        local, mesh=mesh, in_specs=placed,
        out_specs=P("mesh", "blk", None, None, None), check_vma=False,
    )
```

profile of v0, /device:TPU:1, one launch (start us, length us, event | category | flops | bytes accessed | tf_op | source)
XLA Modules:
  0.0 41.6 jit_solution(2086314022777594678)
XLA Ops:
  0.0 0.0 copy-start
  0.7 0.1 copy-done
  0.7 40.1 %conditional.1 = (f32[1,1,4,128,256]{4,3,2,1,0:T(8,128)S(1)}) conditional(s32[]{:T(128)} %bitcast.7, (f32[512,256]{1,0:T(8,128)}, f32[256,256]{1,0:T(8,128)}, f32[128,256]{1,0:T(8,128)}, s32[1,4096]{1,0:T(1,128)S(1)}, f32[1,12288]{1,0:T(1,128)}, /*index=5*/s32[1,4096]{1,0:T(1,128)}) %tuple.83, (f32[512,256]{1,0:T(8,128)}, ...), branch_computations={%region_0.1_spmd, %region_1.2_spmd, %region_2.3_spmd, %region_3.4_... | conditional | bytes 8 | solution.py:375
  0.9 39.5 %rotor_step_5.1 = f32[512,256]{1,0:T(8,128)S(1)} custom-call(f32[512,256]{1,0:T(8,128)} %get-tuple-element.122.fs, f32[256,256]{1,0:T(8,128)} %get-tuple-element.123.kap, f32[128,256]{1,0:T(8,128)} %get-tuple-element.124.st, s32[1,4096]{1,0:T(1,128)S(1)} %get-tuple-element.125.db, f32[1,12288]{1,0:T(1,128)} %get-tuple-element.126.df, ...), custom_call_target="tpu_custom_call" | custom-call | tf_op jit(solution)/shard_map/cond/branch_4_fun/rotor_step_5/pallas_call | solution.py:339
  40.8 0.8 %copy.24 = f32[1,1,4,128,256]{4,3,2,1,0:T(8,128)} copy(f32[1,1,4,128,256]{4,3,2,1,0:T(8,128)S(1)} %get-tuple-element.140) | data formatting | bytes 1048576
Async XLA Ops:
  0.0 0.7 %copy-start = (s32[1,1,4096]{2,1,0:T(1,128)S(1)}, s32[1,1,4096]{2,1,0:T(1,128)}, u32[]{:S(2)}) copy-start(s32[1,1,4096]{2,1,0:T(1,128)} %param.18) | copy-start | bytes 49156
where the time goes:
time: 41.6 us
  Pallas kernels  39.5 us (95%)
  local copies, waits for them, and re-layouts  0.86 us (2%)
  between operations  0.68 us (2%)
  loops' own time  0.55 us (1%)
    pallas_call x1, Pallas kernels, step(): pl.pallas_call(functools.partial(kernel, rot, n), out_shape=jax.ShapeDtyp...  39.5 us
    unnamed x3, local copies, waits for them, and re-layouts  0.86 us

commit v1 on v0

v1 whole, which is shorter than its diff:
```python
import functools

import jax
import jax.numpy as jnp
from jax import lax
from jax.experimental import pallas as pl
from jax.experimental.pallas import tpu as pltpu
from jax.sharding import PartitionSpec as P

CX, CY, CZ = 8, 32, 128
PLANE = CX * CY
ITERS = 2
TURN_MOST = 7
CAP = 64
TILE = 1024
SIDE = 4
GROUPS = sorted(
    ((dy, dx) for dy in range(SIDE) for dx in range(SIDE)),
    key=lambda o: -sum(min(a, SIDE - a) for a in o),
)
ALONG_Z = (2, 1, 3, 0)
OPEN = 2
GROUP = SIDE * CAP


def packed(values):
    word = sum(v << (2 * i) for i, v in enumerate(values))
    return word - (1 << 32) if word >= 1 << 31 else word

LANES = 128
PITCH = 132
MESH = pl.DeviceIdType.MESH
BF = jnp.bfloat16
F32 = jnp.float32


def iota(shape, dim):
    return lax.broadcasted_iota(jnp.int32, shape, dim)


def kernel(
    rot, n,
    fs, kap, st, db, df, fc, out,
    F0, KV, SV, SB, SF, SC, A3, WH, WL, WZ, ZO, QO, QV, E, NN, V2,
    EP, CS, IN, R, G, D, V, FR, NS, VE, GOT, MID,
    sendS, recvS, sendH, recvH,
    in_sem, s_sem, r_sem, hs_sem, hr_sem, m_sem,
):
    m = lax.axis_index("mesh")
    d = lax.axis_index("blk")
    slots = n * CAP
    tiles = slots // TILE
    moved = m == 1

    def near(delta):
        return (d + delta) & (n - 1)

    loads = [
        pltpu.make_async_copy(src, dst, in_sem.at[i])
        for i, (src, dst) in enumerate(
            ((db, SB), (df, SF), (fc, SC.at[0]), (fs, F0), (kap, KV.at[0]), (st, SV.at[0]))
        )
    ]
    for copy in loads:
        copy.start()

    py = [(((d >> 4) + o) & 3) << 4 for o in range(SIDE)]
    px = [(((d >> 2) + o) & 3) << 2 for o in range(SIDE)]
    pz = [(d + o) & 3 for o in range(SIDE)]
    barrier = pltpu.get_barrier_semaphore()
    for dy, dx in GROUPS:
        for dz in ALONG_Z:
            pl.semaphore_signal(barrier, inc=1, device_id=(1 - m, py[dy] + px[dx] + pz[dz]), device_id_type=MESH)
    deltas = sorted({s * k for s in (1, -1) for k in (1, rot, rot + 1, rot - 1) if k})
    for delta in deltas:
        pl.semaphore_signal(barrier, inc=1, device_id=(m, near(delta)), device_id_type=MESH)

    for copy in loads[:3]:
        copy.wait()
    turn = (slots - rot * CAP) % slots

    def turned(x):
        return jnp.where(m == 0, pltpu.roll(x, turn, axis=1), x)

    SB[...] = turned(SB[...])
    SC[0] = turned(SC[0])
    for i in range(3):
        SF[:, i * slots : (i + 1) * slots] = turned(SF[:, i * slots : (i + 1) * slots])

    def hat(count, at, frac):
        i = iota((count, GROUP), 0)
        return jnp.where(i == at, 1.0 - frac, jnp.where(i == at + 1, frac, 0.0))

    def weigh(g):
        cols = pl.ds(pl.multiple_of(g * GROUP, GROUP), GROUP)
        b = SB[:, cols]
        fz, fx, fy = (SF[:, pl.ds(pl.multiple_of(i * slots + g * GROUP, GROUP), GROUP)] for i in range(3))
        hx, hy = hat(CX, (b >> 5) & 7, fx), hat(CY, b & 31, fy)
        for i in range(CX):
            w = hx[i : i + 1] * hy
            hi = w.astype(BF)
            WH[i * CY : (i + 1) * CY, cols] = hi
            WL[i * CY : (i + 1) * CY, cols] = (w - hi.astype(F32)).astype(BF)
        WZ[:, cols] = hat(CZ, b >> 8, fz)

    def split(h, x):
        hi = x.astype(BF)
        A3[:, h * LANES : (h + 1) * LANES] = hi
        A3[:, PLANE + h * LANES : PLANE + (h + 1) * LANES] = (x - hi.astype(F32)).astype(BF)
        A3[:, 2 * PLANE + h * LANES : 2 * PLANE + (h + 1) * LANES] = hi

    lane1 = iota((CZ, LANES), 1)
    y4 = lane1 & 31
    fringe = (y4 == 0) | (y4 == CY - 1)

    def pack(it, get):
        sl, sr = get(0, 0), pltpu.roll(get(1, 0), 32, axis=1)
        for f in range(1, 4):
            here = (lane1 >> 5) == f
            sl = jnp.where(here, pltpu.roll(get(0, f), 32 * f, axis=1), sl)
            sr = jnp.where(here, pltpu.roll(get(1, f), (32 * f + 32) % 128, axis=1), sr)
        sendH[it, 0] = sl
        sendH[it, 1] = sr

    def rows_of(h, f):
        return slice((h * 4 + f) * PITCH, (h * 4 + f) * PITCH + CZ)

    BLOCKS = [(h, f) for h in range(2) for f in range(4)]

    def at(z):
        return pl.ds(z, 8, stride=PITCH)

    top, low = CZ // 2 - 1, CZ // 2

    def solve(V):
        def forward(i, carry):
            a, b = carry
            for u in range(8):
                z = i * 8 + u
                a = (R[at(z)] + a) * G[at(z)]
                b = (R[at(CZ - 1 - z)] + b) * G[at(CZ - 1 - z)]
                D[at(z)] = a
                D[at(CZ - 1 - z)] = b
            return a, b

        zero = jnp.zeros((8, LANES), F32)
        a, b = lax.fori_loop(0, CZ // 16, forward, (zero, zero))
        a = (a + G[at(top)] * b) * MID[...]
        b = b + G[at(low)] * a
        V[at(top)] = a
        V[at(low)] = b

        def backward(i, carry):
            a, b = carry
            for u in range(9):
                z = i * 9 + u + 1
                a = D[at(top - z)] + G[at(top - z)] * a
                b = D[at(low + z)] + G[at(low + z)] * b
                V[at(top - z)] = a
                V[at(low + z)] = b
            return a, b

        lax.fori_loop(0, 7, backward, (a, b))

    def from_within():
        NS[...] = jnp.dot(A3[:, : 2 * PLANE], NN[...], preferred_element_type=F32)
        for h, f in BLOCKS:
            x = NS[f * CZ : (f + 1) * CZ, h * LANES : (h + 1) * LANES]
            R[rows_of(h, f)] = IN[rows_of(h, f)] + CS[rows_of(h, f)] * x

    loads[3].wait()
    pack(0, lambda h, f: F0[f * CZ : (f + 1) * CZ, h * LANES : (h + 1) * LANES])
    for h in range(2):
        split(h, F0[:, h * LANES : (h + 1) * LANES])

    early = pltpu.make_async_remote_copy(
        src_ref=VE, dst_ref=GOT, send_sem=m_sem.at[0], recv_sem=m_sem.at[1],
        device_id=(m, near(rot)), device_id_type=MESH,
    )
    stay = pltpu.make_async_copy(VE, GOT, m_sem.at[2])
    carried = [
        pltpu.make_async_remote_copy(
            src_ref=ref.at[0], dst_ref=ref.at[1], send_sem=m_sem.at[3 + 2 * i], recv_sem=m_sem.at[4 + 2 * i],
            device_id=(m, near(rot)), device_id_type=MESH,
        )
        for i, ref in enumerate((KV, SV, SC))
    ]

    @pl.loop(0, ITERS)
    def _(it):
        ahead = (it > 0) & moved
        edge = [(sendH.at[it, e], recvH.at[it, e]) for e in range(2)]

        def halo(e, delta):
            return pltpu.make_async_remote_copy(
                src_ref=edge[e][0], dst_ref=edge[e][1],
                send_sem=hs_sem.at[it, e], recv_sem=hr_sem.at[it, e],
                device_id=(m, near(delta)), device_id_type=MESH,
            )

        @pl.when(it > 0)
        def _():
            from_within()
            for k in range(8):
                VE[k * PITCH + CZ : (k + 1) * PITCH] = jnp.zeros((PITCH - CZ, LANES), F32)
            solve(VE)
            R[...] = jnp.zeros_like(R)

        def group(k):
            dy, dx = (packed([g[0] for g in GROUPS]) >> (2 * k)) & 3, (packed([g[1] for g in GROUPS]) >> (2 * k)) & 3
            return ((((d >> 4) + dy) & 3) << 2) + (((d >> 2) + dx) & 3)

        per = TILE // GROUP
        shift = jnp.where((it > 0) & (m == 0), rot, 0)

        def send(t):
            for j in range(per):
                g = group(t * per + j)
                for dz in ALONG_Z:
                    pltpu.make_async_remote_copy(
                        src_ref=sendS.at[it, dz % 2, g * 2 + (pz[dz] >> 1)], dst_ref=recvS.at[it, d],
                        send_sem=s_sem.at[it], recv_sem=r_sem.at[it],
                        device_id=(1 - m, (g * SIDE + pz[dz] + shift) & (n - 1)), device_id_type=MESH,
                    ).start()

        @pl.loop(0, tiles)
        def _(t):
            @pl.when((it == 0) & (t == OPEN))
            def _():
                pl.semaphore_wait(barrier, n + len(deltas))

                @pl.loop(0, OPEN - 1)
                def _(u):
                    send(u)

            begin = t == jnp.where(it == 0, OPEN, 0)

            @pl.when(begin & jnp.logical_not(ahead))
            def _():
                halo(0, -1).start()
                halo(1, 1).start()

            @pl.when(begin & ahead)
            def _():
                if rot == 1:
                    pltpu.make_async_copy(edge[0][0], edge[0][1], hr_sem.at[it, 0]).start()
                else:
                    halo(0, rot - 1).start()
                halo(1, rot + 1).start()

            @pl.when(begin & (it > 0) & (m == 0))
            def _():
                stay.start()

            @pl.when(((it > 0) & (t > 0)) | (t >= OPEN))
            def _():
                send(t - 1)

            @pl.when(ahead)
            def _():
                for u in range(2):
                    rows = pl.ds((t * 2 + u) * PITCH, PITCH)
                    pltpu.make_async_remote_copy(
                        src_ref=VE.at[rows], dst_ref=GOT.at[rows], send_sem=m_sem.at[0], recv_sem=m_sem.at[1],
                        device_id=(m, near(rot)), device_id_type=MESH,
                    ).start()

            @pl.when(it == 0)
            def _():
                @pl.loop(0, per)
                def _(j):
                    weigh(group(t * per + j))

            cols = [pl.ds(pl.multiple_of(group(t * per + j) * GROUP, GROUP), GROUP) for j in range(per)]

            def gathered(ref):
                return jnp.concatenate([ref[:, c] for c in cols], axis=1)

            wh = gathered(WH)
            p = jnp.dot(A3[...], jnp.concatenate([wh, wh, gathered(WL)], axis=0), preferred_element_type=F32)
            s = jnp.sum(p.reshape(4, CZ, TILE) * gathered(WZ)[None], axis=1)
            for j in range(per):
                g = group(t * per + j)
                for i in range(2):
                    x = s[:, j * GROUP + i * LANES : j * GROUP + (i + 1) * LANES]
                    sendS[it, 0, g * 2 + i] = x
                    sendS[it, 1, g * 2 + i] = pltpu.roll(x, CAP, axis=1)

        send(tiles - 1)

        @pl.when(it == 0)
        def _():
            loads[4].wait()
            loads[5].wait()

        @pl.when((it == 0) & moved)
        def _():
            for copy in carried:
                copy.start()

        @pl.when(it == 0)
        def _():
            row, col = iota((128, 2 * 2 * 4 * LANES), 0), iota((128, 2 * 2 * 4 * LANES), 1)
            q = row & 15
            kind, half, fld, lane = col >> 10, (col >> 9) & 1, (col >> 7) & 3, col & 127
            place = (q >> 1) * CY + (q & 1) * (CY - 1) + kind * (1 - 2 * (q & 1))
            E[...] = jnp.where((((row >> 4) & 3) == fld) & (half * LANES + lane == place), 1.0, 0.0).astype(BF)
            src, dst = iota((512, 256), 0) & 255, iota((512, 256), 1)
            gap = jnp.abs(src - dst)
            sy, dy = src & 31, dst & 31
            rim = (sy == 0) | (sy == CY - 1) | (dy == 0) | (dy == CY - 1)
            NN[...] = jnp.where(((gap == 1) | (gap == CY)) & ~rim, 1.0, 0.0).astype(BF)

        @pl.when(ahead)
        def _():
            for copy in carried:
                copy.wait()

        @pl.when((it == 0) | moved)
        def _():
            @pl.loop(0, n // SIDE)
            def _(g):
                cols = pl.ds(pl.multiple_of(g * GROUP, GROUP), GROUP)
                c = SC[it, :, cols]
                ZO[:, cols] = jnp.where(iota((CZ, GROUP), 0) == (c >> 8), 1.0, 0.0).astype(BF)
                cq = ((c >> 5) & 7) * 2 + jnp.where((c & 31) == 0, 0, 1)
                QO[:, cols] = jnp.where(iota((16, GROUP), 0) == cq, 1.0, 0.0)

            for h in range(2):
                lanes = slice(h * LANES, (h + 1) * LANES)
                inv = 1.0 / SV[it, :, lanes]
                for f in range(4):
                    k = f // 3
                    c = KV[it, k * CZ : (k + 1) * CZ, lanes]
                    EP[rows_of(h, f)] = (1.0 + 4.0 * c) * inv
                    CS[rows_of(h, f)] = c * inv
                    IN[rows_of(h, f)] = F0[f * CZ : (f + 1) * CZ, lanes] * inv

            def factor(i, carry):
                ha, hb = carry
                for u in range(8):
                    z = i * 8 + u
                    ta, tb = EP[at(z)] + ha, EP[at(CZ - 1 - z)] + hb
                    ga, gb = 1.0 / (1.0 + ta), 1.0 / (1.0 + tb)
                    G[at(z)] = ga
                    G[at(CZ - 1 - z)] = gb
                    ha, hb = ta * ga, tb * gb
                return ha, hb

            one = jnp.ones((8, LANES), F32)
            ha, hb = lax.fori_loop(0, CZ // 16, factor, (one, one))
            MID[...] = 1.0 / (ha + hb - ha * hb)

        @pl.when(it == 0)
        def _():
            from_within()

        for e in range(2):
            halo(e, 1).wait_recv()
        halo(1, 1).wait_send()
        if rot == 1:

            @pl.when(jnp.logical_not(ahead))
            def _():
                halo(0, 1).wait_send()
        else:
            halo(0, 1).wait_send()
        hr, hl = recvH[it, 0], recvH[it, 1]
        for h, f in BLOCKS:
            if h == 0:
                x = jnp.where(lane1 < 32, pltpu.roll(hl, (128 - 32 * f) % 128, axis=1), 0.0)
            else:
                x = jnp.where(lane1 >= 96, pltpu.roll(hr, 96 - 32 * f, axis=1), 0.0)
            R[rows_of(h, f)] = R[rows_of(h, f)] + CS[rows_of(h, f)] * x

        pltpu.make_async_copy(recvS.at[it], recvS.at[it], r_sem.at[it]).wait()
        got = recvS[it].reshape(n // 2, 2, 4, LANES)
        v = jnp.where(iota((n // 2, 4, LANES), 2) < CAP, got[:, 0], got[:, 1])
        for i in range(n // 2):
            V2[:, i * LANES : (i + 1) * LANES] = v[i]
        rest = V2[...]
        for piece in range(2):
            part = rest.astype(BF).astype(F32)
            rest = rest - part
            for f in range(4):
                QV[piece * 64 + f * 16 : piece * 64 + f * 16 + 16, :] = (QO[...] * part[f : f + 1]).astype(BF)
        dp = lax.dot_general(ZO[...], QV[...], (((1,), (1,)), ((), ())), preferred_element_type=F32).astype(BF)
        for h in range(2):
            fr = jnp.dot(dp, E[:, h * 512 : (h + 1) * 512], preferred_element_type=F32)
            nb = jnp.dot(dp, E[:, 1024 + h * 512 : 1024 + (h + 1) * 512], preferred_element_type=F32)
            for f in range(4):
                FR[rows_of(h, f)] = fr[:, f * LANES : (f + 1) * LANES]
                R[rows_of(h, f)] = R[rows_of(h, f)] + CS[rows_of(h, f)] * nb[:, f * LANES : (f + 1) * LANES]
        solve(V)

        pltpu.make_async_copy(recvS.at[it], recvS.at[it], s_sem.at[it]).wait()

        @pl.when(it < ITERS - 1)
        def _():
            def new(h, f):
                return jnp.where(fringe, FR[rows_of(h, f)], V[rows_of(h, f)])

            pack(it + 1, new)
            for h in range(2):
                split(h, jnp.concatenate([new(h, f) for f in range(4)], axis=0))

    @pl.when(m == 0)
    def _():
        stay.wait()

    @pl.when(moved)
    def _():
        early.wait()

    for h, f in BLOCKS:
        out[f * CZ : (f + 1) * CZ, h * LANES : (h + 1) * LANES] = jnp.where(
            fringe, FR[rows_of(h, f)], V[rows_of(h, f)] + GOT[rows_of(h, f)]
        )


def step(rot, n, args):
    slots = n * CAP
    vm = pltpu.VMEM
    dma = pltpu.SemaphoreType.DMA
    tall = vm((8 * PITCH, LANES), F32)
    return pl.pallas_call(
        functools.partial(kernel, rot, n),
        out_shape=jax.ShapeDtypeStruct((4 * CZ, PLANE), F32),
        in_specs=[pl.BlockSpec(memory_space=pl.ANY)] * 6,
        out_specs=pl.BlockSpec(memory_space=pltpu.VMEM),
        scratch_shapes=[
            vm((512, 256), F32), vm((2, 256, 256), F32), vm((2, 128, 256), F32),
            vm((1, slots), jnp.int32), vm((1, 3 * slots), F32), vm((2, 1, slots), jnp.int32),
            vm((512, 768), BF), vm((256, slots), BF), vm((256, slots), BF), vm((CZ, slots), F32), vm((CZ, slots), BF),
            vm((16, slots), F32), vm((128, slots), BF), vm((128, 2048), BF), vm((512, 256), BF),
            vm((4, slots), F32),
            tall, tall, tall, tall, tall, tall, tall, tall,
            vm((512, 256), F32), tall, tall, vm((8, LANES), F32),
            vm((ITERS, 2, n // 2, 4, LANES), F32), vm((ITERS, n, 4, LANES), F32),
            vm((ITERS, 2, CZ, LANES), F32), vm((ITERS, 2, CZ, LANES), F32),
            dma((6,)), dma((ITERS,)), dma((ITERS,)), dma((ITERS, 2)), dma((ITERS, 2)), dma((9,)),
        ],
        compiler_params=pltpu.CompilerParams(collective_id=rot, has_side_effects=True),
        name=f"rotor_step_{rot}",
    )(*args)


def solution(mesh):
    n = mesh.shape["blk"]

    def local(rotation_step, field_state, diffusivity, stretch, donor_base, donor_frac, fringe_cell):
        slots = n * CAP
        args = (
            field_state.reshape(4 * CZ, PLANE),
            diffusivity.reshape(2 * CZ, PLANE),
            stretch.reshape(CZ, PLANE),
            donor_base.reshape(1, slots),
            donor_frac.reshape(1, 3 * slots),
            fringe_cell.reshape(1, slots),
        )
        branches = [functools.partial(lambda rot, a: step(rot, n, a), rot) for rot in range(1, TURN_MOST + 1)]
        new = lax.switch(jnp.clip(rotation_step[0] - 1, 0, TURN_MOST - 1), branches, args)
        return new.reshape(1, 1, 4, CZ, PLANE)

    placed = (
        P(),
        P("mesh", "blk", None, None, None),
        P("mesh", "blk", None, None, None),
        P("mesh", "blk", None, None),
        P("mesh", "blk", None),
        P("mesh", "blk", None, None),
        P("mesh", "blk", None),
    )
    return jax.shard_map(
        local, mesh=mesh, in_specs=placed,
        out_specs=P("mesh", "blk", None, None, None), check_vma=False,
    )
```

time: 41.6 us -> 38.4 us (0.923)
  Pallas kernels: 39.5 us -> 35.8 us
    pallas_call x1, Pallas kernels: 39.5 us -> 35.8 us  [step(): pl.pallas_call(functools.partial(kernel, rot, n), out_shape=jax.ShapeDtyp...]
where the time goes in v1:
time: 38.4 us; the launch traced here: 38.1 us
  Pallas kernels  35.8 us (93%)
  local copies, waits for them, and re-layouts  0.86 us (2%)
  loops' own time  0.77 us (2%)
  between operations  0.68 us (2%)
    pallas_call x1, Pallas kernels, step(): pl.pallas_call(functools.partial(kernel, rot, n), out_shape=jax.ShapeDtyp...  35.8 us
    unnamed x3, local copies, waits for them, and re-layouts  0.86 us
    another operation x1, loops' own time, local(): lax.switch(jnp.clip(rotation_step[0] - 1, 0, TURN_MOST - 1), branches, args)  0.77 us

profile of v1, /device:TPU:1, one launch (start us, length us, event | category | flops | bytes accessed | tf_op | source)
XLA Modules:
  0.0 38.1 jit_solution(17722118851756860223)
XLA Ops:
  0.0 0.0 copy-start
  0.7 0.1 copy-done
  0.7 36.5 %conditional.1 = (f32[1,1,4,128,256]{4,3,2,1,0:T(8,128)S(1)}) conditional(s32[]{:T(128)} %bitcast.7, (f32[512,256]{1,0:T(8,128)}, f32[256,256]{1,0:T(8,128)}, f32[128,256]{1,0:T(8,128)}, s32[1,4096]{1,0:T(1,128)S(1)}, f32[1,12288]{1,0:T(1,128)}, /*index=5*/s32[1,4096]{1,0:T(1,128)}) %tuple.83, (f32[512,256]{1,0:T(8,128)}, ...), branch_computations={%region_0.1_spmd, %region_1.2_spmd, %region_2.3_spmd, %region_3.4_... | conditional | bytes 8 | solution.py:462
  1.2 35.8 %rotor_step_7.1 = f32[512,256]{1,0:T(8,128)S(1)} custom-call(f32[512,256]{1,0:T(8,128)} %get-tuple-element.134.fs, f32[256,256]{1,0:T(8,128)} %get-tuple-element.135.kap, f32[128,256]{1,0:T(8,128)} %get-tuple-element.136.st, s32[1,4096]{1,0:T(1,128)S(1)} %get-tuple-element.137.db, f32[1,12288]{1,0:T(1,128)} %get-tuple-element.138.df, ...), custom_call_target="tpu_custom_call" | custom-call | tf_op jit(solution)/shard_map/cond/branch_6_fun/rotor_step_7/pallas_call | solution.py:426
  37.3 0.8 %copy.24 = f32[1,1,4,128,256]{4,3,2,1,0:T(8,128)} copy(f32[1,1,4,128,256]{4,3,2,1,0:T(8,128)S(1)} %get-tuple-element.140) | data formatting | bytes 1048576
Async XLA Ops:
  0.0 0.7 %copy-start = (s32[1,1,4096]{2,1,0:T(1,128)S(1)}, s32[1,1,4096]{2,1,0:T(1,128)}, u32[]{:S(2)}) copy-start(s32[1,1,4096]{2,1,0:T(1,128)} %param.18) | copy-start | bytes 49156

commit v2 on v1

--- a/solution.py
+++ b/solution.py
@@ -20,6 +20,7 @@
 )
 ALONG_Z = (2, 1, 3, 0)
 OPEN = 2
+CHUNKS = 0x64210
 GROUP = SIDE * CAP
 
 
@@ -42,7 +43,7 @@
     rot, n,
     fs, kap, st, db, df, fc, out,
     F0, KV, SV, SB, SF, SC, A3, WH, WL, WZ, ZO, QO, QV, E, NN, V2,
-    EP, CS, IN, R, G, D, V, FR, NS, VE, GOT, MID,
+    EP, CS, IN, R, G, D, V, FR, NS, VE, GOT, MID, CARRY,
     sendS, recvS, sendH, recvH,
     in_sem, s_sem, r_sem, hs_sem, hr_sem, m_sem,
 ):
@@ -177,14 +178,37 @@
         src_ref=VE, dst_ref=GOT, send_sem=m_sem.at[0], recv_sem=m_sem.at[1],
         device_id=(m, near(rot)), device_id_type=MESH,
     )
-    stay = pltpu.make_async_copy(VE, GOT, m_sem.at[2])
     carried = [
         pltpu.make_async_remote_copy(
-            src_ref=ref.at[0], dst_ref=ref.at[1], send_sem=m_sem.at[3 + 2 * i], recv_sem=m_sem.at[4 + 2 * i],
+            src_ref=src, dst_ref=dst, send_sem=m_sem.at[2 + 2 * i], recv_sem=m_sem.at[3 + 2 * i],
             device_id=(m, near(rot)), device_id_type=MESH,
         )
-        for i, ref in enumerate((KV, SV, SC))
+        for i, (src, dst) in enumerate(((SC.at[0], SC.at[1]), *((CARRY.at[k], CARRY.at[3 + k]) for k in range(3))))
     ]
+
+    def packing(h):
+        c = lane1 & 63
+        inner = (((c - 32) >> 1) + (1 - h)) * CY + jnp.where(c & 1 == 0, 1, CY - 2)
+        return jnp.where(c < 32, c + 96 * h, inner & 127)
+
+    def unpacking(h):
+        x, y = lane1 >> 5, lane1 & 31
+        outer = x == 3 * h
+        place = jnp.where(outer, y, 32 + (x - (1 - h)) * 2 + (y >> 4)) + 64 * h
+        return place & 127, outer | (y == 1) | (y == CY - 2)
+
+    def gather(x, index):
+        return jnp.take_along_axis(x, index, axis=1, mode="promise_in_bounds")
+
+    planes = [(KV, 0, 1.0), (KV, CZ, 1.0), (SV, 0, 1000.0)]
+
+    @pl.when(moved)
+    def _():
+        for copy in loads[4:]:
+            copy.wait()
+        for k, (ref, r, _) in enumerate(planes):
+            a, b = (gather(ref[0, r : r + CZ, h * LANES : (h + 1) * LANES], packing(h)) for h in range(2))
+            CARRY[k] = jnp.where(lane1 < 64, a, b)
 
     @pl.loop(0, ITERS)
     def _(it):
@@ -198,7 +222,7 @@
                 device_id=(m, near(delta)), device_id_type=MESH,
             )
 
-        @pl.when(it > 0)
+        @pl.when(ahead)
         def _():
             from_within()
             for k in range(8):
@@ -206,6 +230,16 @@
             solve(VE)
             R[...] = jnp.zeros_like(R)
 
+        def part(u):
+            rows = pl.ds(u * PITCH, PITCH)
+            return pltpu.make_async_remote_copy(
+                src_ref=VE.at[rows], dst_ref=GOT.at[rows], send_sem=m_sem.at[0], recv_sem=m_sem.at[1],
+                device_id=(m, near(rot)), device_id_type=MESH,
+            )
+
+        def chunk_at(t):
+            return (CHUNKS >> (4 * t)) & 15
+
         def group(k):
             dy, dx = (packed([g[0] for g in GROUPS]) >> (2 * k)) & 3, (packed([g[1] for g in GROUPS]) >> (2 * k)) & 3
             return ((((d >> 4) + dy) & 3) << 2) + (((d >> 2) + dx) & 3)
@@ -218,7 +252,7 @@
                 g = group(t * per + j)
                 for dz in ALONG_Z:
                     pltpu.make_async_remote_copy(
-                        src_ref=sendS.at[it, dz % 2, g * 2 + (pz[dz] >> 1)], dst_ref=recvS.at[it, d],
+                        src_ref=sendS.at[it, pz[dz] & 1, g * 2 + (pz[dz] >> 1)], dst_ref=recvS.at[it, d],
                         send_sem=s_sem.at[it], recv_sem=r_sem.at[it],
                         device_id=(1 - m, (g * SIDE + pz[dz] + shift) & (n - 1)), device_id_type=MESH,
                     ).start()
@@ -248,22 +282,24 @@
                     halo(0, rot - 1).start()
                 halo(1, rot + 1).start()
 
-            @pl.when(begin & (it > 0) & (m == 0))
-            def _():
-                stay.start()
-
             @pl.when(((it > 0) & (t > 0)) | (t >= OPEN))
             def _():
                 send(t - 1)
 
+            @pl.when((it == 0) & (t == OPEN) & moved)
+            def _():
+                carried[0].start()
+                carried[1].start()
+
+            @pl.when((it == 0) & (t == OPEN + 1) & moved)
+            def _():
+                carried[2].start()
+
             @pl.when(ahead)
             def _():
-                for u in range(2):
-                    rows = pl.ds((t * 2 + u) * PITCH, PITCH)
-                    pltpu.make_async_remote_copy(
-                        src_ref=VE.at[rows], dst_ref=GOT.at[rows], send_sem=m_sem.at[0], recv_sem=m_sem.at[1],
-                        device_id=(m, near(rot)), device_id_type=MESH,
-                    ).start()
+                @pl.loop(chunk_at(t), chunk_at(t + 1))
+                def _(u):
+                    part(u).start()
 
             @pl.when(it == 0)
             def _():
@@ -279,24 +315,32 @@
             wh = gathered(WH)
             p = jnp.dot(A3[...], jnp.concatenate([wh, wh, gathered(WL)], axis=0), preferred_element_type=F32)
             s = jnp.sum(p.reshape(4, CZ, TILE) * gathered(WZ)[None], axis=1)
+            first = iota((2, LANES), 1) < CAP
             for j in range(per):
                 g = group(t * per + j)
                 for i in range(2):
                     x = s[:, j * GROUP + i * LANES : j * GROUP + (i + 1) * LANES]
-                    sendS[it, 0, g * 2 + i] = x
-                    sendS[it, 1, g * 2 + i] = pltpu.roll(x, CAP, axis=1)
+                    y = pltpu.roll(x, CAP, axis=1)
+                    sendS[it, 0, g * 2 + i] = jnp.where(first, x[:2], y[2:])
+                    sendS[it, 1, g * 2 + i] = jnp.where(first, y[:2], x[2:])
 
         send(tiles - 1)
 
-        @pl.when(it == 0)
-        def _():
-            loads[4].wait()
-            loads[5].wait()
+        @pl.when(ahead)
+        def _():
+            @pl.loop(chunk_at(tiles), 8)
+            def _(u):
+                part(u).start()
 
         @pl.when((it == 0) & moved)
         def _():
-            for copy in carried:
-                copy.start()
+            carried[3].start()
+
+        @pl.when((it == 0) & (m == 0))
+        def _():
+            for copy in loads[4:]:
+                copy.wait()
+            GOT[...] = jnp.zeros_like(GOT)
 
         @pl.when(it == 0)
         def _():
@@ -315,6 +359,10 @@
         def _():
             for copy in carried:
                 copy.wait()
+            for k, (ref, r, other) in enumerate(planes):
+                for h in range(2):
+                    index, used = unpacking(h)
+                    ref[1, r : r + CZ, h * LANES : (h + 1) * LANES] = jnp.where(used, gather(CARRY[3 + k], index), other)
 
         @pl.when((it == 0) | moved)
         def _():
@@ -351,7 +399,7 @@
             ha, hb = lax.fori_loop(0, CZ // 16, factor, (one, one))
             MID[...] = 1.0 / (ha + hb - ha * hb)
 
-        @pl.when(it == 0)
+        @pl.when(jnp.logical_not(ahead))
         def _():
             from_within()
 
@@ -374,16 +422,21 @@
             R[rows_of(h, f)] = R[rows_of(h, f)] + CS[rows_of(h, f)] * x
 
         pltpu.make_async_copy(recvS.at[it], recvS.at[it], r_sem.at[it]).wait()
-        got = recvS[it].reshape(n // 2, 2, 4, LANES)
-        v = jnp.where(iota((n // 2, 4, LANES), 2) < CAP, got[:, 0], got[:, 1])
-        for i in range(n // 2):
-            V2[:, i * LANES : (i + 1) * LANES] = v[i]
-        rest = V2[...]
+        got = recvS[it].reshape(n // 4, 8, LANES)
+        front = (iota(got.shape, 1) & 2) == 0
+        turned = pltpu.roll(got, CAP, axis=2)
+        turned = jnp.where(front, pltpu.roll(turned, 6, axis=1), pltpu.roll(turned, 2, axis=1))
+        rest = jnp.where((iota(got.shape, 2) < CAP) == front, got, turned).reshape(2 * n, LANES)
         for piece in range(2):
             part = rest.astype(BF).astype(F32)
             rest = rest - part
-            for f in range(4):
-                QV[piece * 64 + f * 16 : piece * 64 + f * 16 + 16, :] = (QO[...] * part[f : f + 1]).astype(BF)
+            V2[piece] = part
+        for i in range(n // 2):
+            cols = slice(i * LANES, (i + 1) * LANES)
+            for piece in range(2):
+                for f in range(4):
+                    r = piece * 64 + f * 16
+                    QV[r : r + 16, cols] = (QO[:, cols] * V2[piece, i * 4 + f : i * 4 + f + 1]).astype(BF)
         dp = lax.dot_general(ZO[...], QV[...], (((1,), (1,)), ((), ())), preferred_element_type=F32).astype(BF)
         for h in range(2):
             fr = jnp.dot(dp, E[:, h * 512 : (h + 1) * 512], preferred_element_type=F32)
@@ -403,10 +456,6 @@
             pack(it + 1, new)
             for h in range(2):
                 split(h, jnp.concatenate([new(h, f) for f in range(4)], axis=0))
-
-    @pl.when(m == 0)
-    def _():
-        stay.wait()
 
     @pl.when(moved)
     def _():
@@ -433,12 +482,12 @@
             vm((1, slots), jnp.int32), vm((1, 3 * slots), F32), vm((2, 1, slots), jnp.int32),
             vm((512, 768), BF), vm((256, slots), BF), vm((256, slots), BF), vm((CZ, slots), F32), vm((CZ, slots), BF),
             vm((16, slots), F32), vm((128, slots), BF), vm((128, 2048), BF), vm((512, 256), BF),
-            vm((4, slots), F32),
+            vm((2, 2 * n, LANES), F32),
             tall, tall, tall, tall, tall, tall, tall, tall,
-            vm((512, 256), F32), tall, tall, vm((8, LANES), F32),
-            vm((ITERS, 2, n // 2, 4, LANES), F32), vm((ITERS, n, 4, LANES), F32),
+            vm((512, 256), F32), tall, tall, vm((8, LANES), F32), vm((6, CZ, LANES), F32),
+            vm((ITERS, 2, n // 2, 2, LANES), F32), vm((ITERS, n, 2, LANES), F32),
             vm((ITERS, 2, CZ, LANES), F32), vm((ITERS, 2, CZ, LANES), F32),
-            dma((6,)), dma((ITERS,)), dma((ITERS,)), dma((ITERS, 2)), dma((ITERS, 2)), dma((9,)),
+            dma((6,)), dma((ITERS,)), dma((ITERS,)), dma((ITERS, 2)), dma((ITERS, 2)), dma((10,)),
         ],
         compiler_params=pltpu.CompilerParams(collective_id=rot, has_side_effects=True),
         name=f"rotor_step_{rot}",

time: 38.4 us -> 33.2 us (0.86)
  Pallas kernels: 35.8 us -> 30.9 us
    pallas_call x1, Pallas kernels: 35.8 us -> 30.9 us  [step(): pl.pallas_call(functools.partial(kernel, rot, n), out_shape=jax.ShapeDtyp...]
where the time goes in v2:
time: 33.2 us; the launch traced here: 33 us
  Pallas kernels  30.9 us (93%)
  local copies, waits for them, and re-layouts  0.86 us (3%)
  between operations  0.68 us (2%)
  loops' own time  0.55 us (2%)
    pallas_call x1, Pallas kernels, step(): pl.pallas_call(functools.partial(kernel, rot, n), out_shape=jax.ShapeDtyp...  30.9 us
    unnamed x3, local copies, waits for them, and re-layouts  0.86 us

profile of v2, /device:TPU:1, one launch (start us, length us, event | category | flops | bytes accessed | tf_op | source)
XLA Modules:
  0.0 33.0 jit_solution(9443102676758032544)
XLA Ops:
  0.0 0.0 copy-start
  0.7 0.1 copy-done
  0.7 31.4 %conditional.1 = (f32[1,1,4,128,256]{4,3,2,1,0:T(8,128)S(1)}) conditional(s32[]{:T(128)} %bitcast.7, (f32[512,256]{1,0:T(8,128)}, f32[256,256]{1,0:T(8,128)}, f32[128,256]{1,0:T(8,128)}, s32[1,4096]{1,0:T(1,128)S(1)}, f32[1,12288]{1,0:T(1,128)}, /*index=5*/s32[1,4096]{1,0:T(1,128)}) %tuple.83, (f32[512,256]{1,0:T(8,128)}, ...), branch_computations={%region_0.1_spmd, %region_1.2_spmd, %region_2.3_spmd, %region_3.4_... | conditional | bytes 8 | solution.py:511
  0.9 30.9 %rotor_step_4.1 = f32[512,256]{1,0:T(8,128)S(1)} custom-call(f32[512,256]{1,0:T(8,128)} %get-tuple-element.116.fs, f32[256,256]{1,0:T(8,128)} %get-tuple-element.117.kap, f32[128,256]{1,0:T(8,128)} %get-tuple-element.118.st, s32[1,4096]{1,0:T(1,128)S(1)} %get-tuple-element.119.db, f32[1,12288]{1,0:T(1,128)} %get-tuple-element.120.df, ...), custom_call_target="tpu_custom_call" | custom-call | tf_op jit(solution)/shard_map/cond/branch_3_fun/rotor_step_4/pallas_call | solution.py:475
  32.2 0.8 %copy.24 = f32[1,1,4,128,256]{4,3,2,1,0:T(8,128)} copy(f32[1,1,4,128,256]{4,3,2,1,0:T(8,128)S(1)} %get-tuple-element.140) | data formatting | bytes 1048576
Async XLA Ops:
  0.0 0.7 %copy-start = (s32[1,1,4096]{2,1,0:T(1,128)S(1)}, s32[1,1,4096]{2,1,0:T(1,128)}, u32[]{:S(2)}) copy-start(s32[1,1,4096]{2,1,0:T(1,128)} %param.18) | copy-start | bytes 49156
